TPU v7x, 512 devices: a whole 4x4x16 slice. The times are simulated.
512 devices in a mesh: view: 8 (over y, x_lo), batch: 64 (over x_hi, z, core).
Axes of the slice: x: 4 (x_hi: 2, x_lo: 2; x = x_hi * 2 + x_lo), y: 4, z: 16, core: 2. Of those that a mesh axis runs over, the one named last changes fastest.
Arguments:
- embeddings: bfloat16 [8, 8192, 256], P('view', 'batch'), may hold values from -1.5 to 1.5
- positive: int32 [8, 8192], P(None, 'batch'), may hold values from 0 to 127, as said below
Outputs:
- gradients: float32 [8, 8192, 256], P('view', 'batch')
- totals: float32 [8, 8192], P('view', 'batch')
- row_loss: float32 [8, 8192], P('view', 'batch')
Inputs may be any that keep to these rules, and one draw needn't show every extreme that they name: `positive`: for each view and each aligned block of 128 samples, the entries are a permutation of 0 to 127.
All inputs are finite; a program needn't handle non-finite values.
Results may differ from a plain program's by a relative error of at most 0.002.
Values may be sent and summed in bfloat16 or wider, within the bound.
No kernel may reach another device: no remote copies, remote signals or barrier semaphores. Data moves between devices by JAX's collectives and lax.ppermute only.
A program may use at most 64 MiB of HBM per device.

v0:
```python
import jax
import jax.numpy as jnp
from jax import lax
from jax.sharding import PartitionSpec as P

logit_scale = 10.0


def from_partner(value, axis, bit):
    return lax.ppermute(value, axis, [(i, i ^ 1 << bit) for i in range(lax.axis_size(axis))])


def body(embeddings, positive):
    own_rows = embeddings[0]
    row_count = own_rows.shape[0]
    view_count = lax.axis_size("view")
    swap_bit = view_count.bit_length() - 2
    partner = from_partner(own_rows, "view", swap_bit)
    view_index = lax.axis_index("view")
    own_match = lax.dynamic_index_in_dim(positive, view_index, 0, keepdims=False)
    far_match = lax.dynamic_index_in_dim(
        positive, jnp.bitwise_xor(view_index, view_count // 2), 0, keepdims=False
    )

    def score_piece(key_piece):
        return (
            jnp.einsum("ie,je->ij", own_rows, key_piece, preferred_element_type=jnp.float32)
            * logit_scale
        )

    running_max = jnp.full((row_count,), -1e30, jnp.float32)
    scores = score_piece(lax.all_gather(partner, "batch", axis=0, tiled=True))
    new_max = jnp.maximum(running_max, jnp.max(scores, axis=1))
    summed = jnp.sum(jnp.exp(scores - new_max[:, None]), axis=1)
    running_max, summed = (new_max, summed)
    totals = running_max + jnp.log(summed)
    far_totals = from_partner(totals, "view", swap_bit)
    every_total = lax.all_gather(far_totals, "batch", axis=0, tiled=True)
    key_piece = lax.all_gather(partner, "batch", axis=0, tiled=True)
    scores = score_piece(key_piece)
    w_rows = jnp.exp(scores - totals[:, None]).astype(jnp.bfloat16)
    w_cols = jnp.exp(scores - every_total[None, :]).astype(jnp.bfloat16)
    products = jnp.dot(
        jnp.concatenate([w_rows, w_cols], axis=0), key_piece, preferred_element_type=jnp.float32
    )
    own_acc = products[:row_count]
    side_acc = products[row_count:]
    spread = own_acc + side_acc
    pos_rows = jnp.take(partner, own_match, axis=0).astype(jnp.float32)
    pos_score = jnp.sum(own_rows.astype(jnp.float32) * pos_rows, axis=1) * logit_scale
    row_loss = totals - pos_score
    row_ids = jnp.arange(row_count, dtype=jnp.int32)
    matched_hot = (far_match[None, :] == row_ids[:, None]).astype(jnp.bfloat16)
    matched = jnp.dot(matched_hot, partner, preferred_element_type=jnp.float32)
    gradients = logit_scale * (spread - pos_rows - matched)
    return (gradients[None], totals[None], row_loss[None])


def solution(mesh):
    return jax.shard_map(
        body,
        mesh=mesh,
        in_specs=(P("view", "batch", None), P(None, "batch")),
        out_specs=(P("view", "batch", None), P("view", "batch"), P("view", "batch")),
        check_vma=False,
    )
```

profile of v0, /device:TPU:1, one launch (start us, length us, event | category | flops | bytes accessed | tf_op | source)
XLA Modules:
  0.0 268.4 jit_solution(11104582229734057468)
XLA Ops:
  7.2 0.0 all-gather.3.cloned.1.call-start
  7.2 5.6 %collective-permute-start = (bf16[128,256]{1,0:T(8,128)(2,1)}, bf16[128,256]{1,0:T(8,128)(2,1)S(1)}, u32[]{:S(2)}, u32[]{:S(2)}) collective-permute-start(bf16[128,256]{1,0:T(8,128)(2,1)} %bitcast.25), channel_id=1, source_target_pairs={{0,256},{64,320},{128,384},{192,448},{256,0},{320,64},{384,128},{4... | collective-permute-start | bytes 196616 | tf_op jit(solution)/shard_map/ppermute | solution.py:10
  12.9 1.9 collective-permute-done
  14.7 0.0 copy-start
  14.7 0.6 copy-done
  15.3 0.0 all-gather.3.cloned.1.call-update
  15.4 0.7 fusion.10
  16.1 0.7 compare_and_fusion
  16.8 0.7 dynamic-slice_bitcast_fusion
  17.5 1.6 gather_fusion
  19.1 1.0 fusion.7
  20.1 152.4 %all-gather.3.cloned.1.call-done = bf16[8192,256]{1,0:T(8,128)(2,1)} async-done(((bf16[128,256]{1,0:T(8,128)(2,1)}), bf16[8192,256]{1,0:T(8,128)(2,1)}) %all-gather.3.cloned.1.call-update) | async-done | bytes 4194320 | tf_op jit(solution)/shard_map/all_gather | solution.py:39
  172.5 3.8 %fusion.13 = (f32[128]{0:T(128)S(1)}, f32[128,8192]{1,0:T(8,128)S(1)}) fusion(bf16[8192,256]{1,0:T(8,128)(2,1)} %all-gather.3.cloned.1.call-done, bf16[1,128,256]{2,1,0:T(8,128)(2,1)} %param.2), kind=kOutput, calls=%fused_computation.32 | convolution fusion | flops 538967936 | bytes 8454656 | tf_op jit(solution)/shard_map/ie,je->ij/dot_general | solution.py:27
  176.3 0.8 exponential_reduce_fusion
  177.0 0.0 copy-start.3
  177.1 4.6 %collective-permute-start.1 = (f32[128]{0:T(128)S(1)}, f32[128]{0:T(128)S(1)}, u32[]{:S(2)}, u32[]{:S(2)}) collective-permute-start(f32[128]{0:T(128)S(1)} %log_add_fusion), channel_id=1, source_target_pairs={{0,256},{64,320},{128,384},{192,448},{256,0},{320,64},{384,128},{4... | collective-permute-start | bytes 1544 | tf_op jit(solution)/shard_map/ppermute | solution.py:10
  181.7 0.5 bitcast_subtract_fusion
  182.2 0.7 collective-permute-done.1
  182.9 74.4 %all-gather = f32[64,1,128]{2,1,0:T(1,128)S(1)} all-gather(f32[1,1,128]{2,1,0:T(1,128)S(1)} %bitcast.28), channel_id=1, replica_groups=mesh['view'=8,'batch'=64] {'batch'}, dimensions={0}, use_global_device_ids=true | all-gather | bytes 33280 | tf_op jit(solution)/shard_map/all_gather | solution.py:38
  257.3 0.0 copy-start.2
  257.3 1.5 exponential_convert_fusion.1
  258.7 0.0 copy-done.3
  258.8 0.7 copy-done.2
  259.5 0.0 copy-start.1
  259.5 1.2 fusion
  260.7 0.0 copy-done.1
  260.7 0.8 fusion.6
  (3 shorter events, 0.0 us)
Async XLA Ops:
  7.2 165.3 %all-gather.3.cloned.1.call-start = ((), (), s32[]{:S(2)}) async-start(), calls=%async_computation | async-start | bytes 4259840 | tf_op jit(solution)/shard_map/all_gather | solution.py:39
  7.2 7.5 %collective-permute-start = (bf16[128,256]{1,0:T(8,128)(2,1)}, bf16[128,256]{1,0:T(8,128)(2,1)S(1)}, u32[]{:S(2)}, u32[]{:S(2)}) collective-permute-start(bf16[128,256]{1,0:T(8,128)(2,1)} %bitcast.25), channel_id=1, source_target_pairs={{0,256},{64,320},{128,384},{192,448},{256,0},{320,64},{384,128},{4... | collective-permute-start | bytes 196616 | tf_op jit(solution)/shard_map/ppermute | solution.py:10
  14.7 0.6 copy-start
  177.0 81.7 %copy-start.3 = (f32[128]{0:T(128)}, f32[128]{0:T(128)S(1)}, u32[]{:S(2)}) copy-start(f32[128]{0:T(128)S(1)} %log_add_fusion) | copy-start | bytes 1540
  177.1 5.8 %collective-permute-start.1 = (f32[128]{0:T(128)S(1)}, f32[128]{0:T(128)S(1)}, u32[]{:S(2)}, u32[]{:S(2)}) collective-permute-start(f32[128]{0:T(128)S(1)} %log_add_fusion), channel_id=1, source_target_pairs={{0,256},{64,320},{128,384},{192,448},{256,0},{320,64},{384,128},{4... | collective-permute-start | bytes 1544 | tf_op jit(solution)/shard_map/ppermute | solution.py:10
  257.3 2.2 copy-start.2
  259.5 1.3 copy-start.1
Sparse Core Ops, SparseCore 0:
  15.5 156.9 all-gather.2
where the time goes:
time: 269 us; the launch traced here: 268 us
  waiting for transfers between devices  155 us (58%)
  blocking collectives  74.4 us (28%)
  between operations  14.1 us (5%)
  starting transfers between devices  10.3 us (4%)
  matrix products  5.86 us (2%)
  other arithmetic  5.15 us (2%)
  local copies, waits for them, and re-layouts  3.66 us (1%)
    all_gather x1, waiting for transfers between devices, body(): key_piece = lax.all_gather(partner, 'batch', axis=0, tiled=True)  152 us
    all_gather x1, blocking collectives, body(): every_total = lax.all_gather(far_totals, 'batch', axis=0, tiled=True)  74.4 us
    ppermute x2, starting transfers between devices, from_partner(): lax.ppermute(value, axis, [(i, i ^ 1 << bit) for i in range(lax.axis_size...  10.3 us
  transfers between devices with their start and end apart: 3, of which 3 were waited for; matrix products, arithmetic and copies ran while one was open for 2% of the time, Pallas kernels for 0%

commit v1 on v0

--- a/solution.py
+++ b/solution.py
@@ -35,7 +35,9 @@
     running_max, summed = (new_max, summed)
     totals = running_max + jnp.log(summed)
     far_totals = from_partner(totals, "view", swap_bit)
-    every_total = lax.all_gather(far_totals, "batch", axis=0, tiled=True)
+    every_total = jnp.concatenate(
+        lax.all_to_all(jnp.stack([far_totals] * lax.axis_size("batch")), "batch", 0, 0), axis=0
+    )
     key_piece = lax.all_gather(partner, "batch", axis=0, tiled=True)
     scores = score_piece(key_piece)
     w_rows = jnp.exp(scores - totals[:, None]).astype(jnp.bfloat16)

time: 269 us -> 222 us (0.83)
  blocking collectives: 74.4 us -> 0 us
  waiting for transfers between devices: 155 us -> 170 us
  starting transfers between devices: 10.3 us -> 19.2 us
    all_gather x1 -> x0, blocking collectives: 74.4 us -> none  [body(): every_total = lax.all_gather(far_totals, 'batch', axis=0, tiled=True)]
    all_to_all x0 -> x1, waiting for transfers between devices: none -> 14.1 us  [body(): lax.all_to_all(jnp.stack([far_totals] * lax.axis_size('batch')), 'batch',...]
    all_to_all x0 -> x1, starting transfers between devices: none -> 8.9 us  [body(): lax.all_to_all(jnp.stack([far_totals] * lax.axis_size('batch')), 'batch',...]
  transfers between devices with their start and end apart: 3 -> 4, of which waited for: 3 -> 4; matrix products, arithmetic and copies ran while one was open for 2% -> 2% of each run, Pallas kernels for 0% -> 0%
where the time goes in v1:
time: 222 us; the launch traced here: 221 us
  waiting for transfers between devices  170 us (77%)
  starting transfers between devices  19.2 us (9%)
  between operations  14.2 us (6%)
  other arithmetic  6.3 us (3%)
  matrix products  5.86 us (3%)
  local copies, waits for them, and re-layouts  5.53 us (2%)
    all_gather x1, waiting for transfers between devices, body(): key_piece = lax.all_gather(partner, 'batch', axis=0, tiled=True)  153 us
    all_to_all x1, waiting for transfers between devices, body(): lax.all_to_all(jnp.stack([far_totals] * lax.axis_size('batch')), 'batch',...  14.1 us
    ppermute x2, starting transfers between devices, from_partner(): lax.ppermute(value, axis, [(i, i ^ 1 << bit) for i in range(lax.axis_size...  10.3 us
    all_to_all x1, starting transfers between devices, body(): lax.all_to_all(jnp.stack([far_totals] * lax.axis_size('batch')), 'batch',...  8.9 us
  transfers between devices with their start and end apart: 4, of which 4 were waited for; matrix products, arithmetic and copies ran while one was open for 2% of the time, Pallas kernels for 0%

profile of v1, /device:TPU:1, one launch (start us, length us, event | category | flops | bytes accessed | tf_op | source)
XLA Modules:
  0.0 221.4 jit_solution(7015144948123884055)
XLA Ops:
  7.2 0.0 all-gather.2.cloned.1.call-start
  7.2 5.6 %collective-permute-start = (bf16[128,256]{1,0:T(8,128)(2,1)}, bf16[128,256]{1,0:T(8,128)(2,1)S(1)}, u32[]{:S(2)}, u32[]{:S(2)}) collective-permute-start(bf16[128,256]{1,0:T(8,128)(2,1)} %bitcast.24), channel_id=1, source_target_pairs={{0,256},{64,320},{128,384},{192,448},{256,0},{320,64},{384,128},{4... | collective-permute-start | bytes 196616 | tf_op jit(solution)/shard_map/ppermute | solution.py:10
  12.9 1.9 collective-permute-done
  14.7 0.0 copy-start.1
  14.7 0.6 copy-done.1
  15.3 0.0 all-gather.2.cloned.1.call-update
  15.4 0.7 fusion.10
  16.1 0.7 compare_and_fusion
  16.8 0.7 dynamic-slice_bitcast_fusion
  17.5 1.6 gather_fusion
  19.1 153.4 %all-gather.2.cloned.1.call-done = bf16[8192,256]{1,0:T(8,128)(2,1)} async-done(((bf16[128,256]{1,0:T(8,128)(2,1)}), bf16[8192,256]{1,0:T(8,128)(2,1)}) %all-gather.2.cloned.1.call-update) | async-done | bytes 4194320 | tf_op jit(solution)/shard_map/all_gather | solution.py:41
  172.5 3.8 %fusion.13 = (f32[128]{0:T(128)S(1)}, f32[128,8192]{1,0:T(8,128)S(1)}) fusion(bf16[8192,256]{1,0:T(8,128)(2,1)} %all-gather.2.cloned.1.call-done, bf16[1,128,256]{2,1,0:T(8,128)(2,1)} %param.2), kind=kOutput, calls=%fused_computation.32 | convolution fusion | flops 538967936 | bytes 8454656 | tf_op jit(solution)/shard_map/ie,je->ij/dot_general | solution.py:27
  176.3 0.0 copy-start
  176.3 0.0 copy-start.4
  176.3 1.9 copy-done
  178.2 0.7 exponential_reduce_fusion
  179.0 0.0 copy-start.5
  179.0 4.6 %collective-permute-start.1 = (f32[128]{0:T(128)S(1)}, f32[128]{0:T(128)S(1)}, u32[]{:S(2)}, u32[]{:S(2)}) collective-permute-start(f32[128]{0:T(128)S(1)} %log_add_fusion), channel_id=1, source_target_pairs={{0,256},{64,320},{128,384},{192,448},{256,0},{320,64},{384,128},{4... | collective-permute-start | bytes 1544 | tf_op jit(solution)/shard_map/ppermute | solution.py:10
  183.7 0.0 copy-done.4
  183.7 0.2 fusion.7
  183.8 1.0 collective-permute-done.1
  184.8 0.6 stack.2
  185.5 8.9 %all-to-all-start = ((f32[64,1,128]{2,1,0:T(1,128)}), f32[64,1,128]{2,1,0:T(1,128)S(1)}, u32[]{:S(2)}, u32[]{:S(2)}) async-start(f32[64,1,128]{2,1,0:T(1,128)} %stack.2), calls=%async_computation | async-start | bytes 65536 | tf_op jit(solution)/shard_map/all_to_all | solution.py:39
  194.4 0.5 bitcast_subtract_fusion
  194.9 14.1 %all-to-all-done = f32[64,1,128]{2,1,0:T(1,128)S(1)} async-done(((f32[64,1,128]{2,1,0:T(1,128)}), f32[64,1,128]{2,1,0:T(1,128)S(1)}, u32[]{:S(2)}, u32[]{:S(2)}) %all-to-all-start) | async-done | bytes 32800 | tf_op jit(solution)/shard_map/all_to_all | solution.py:39
  209.0 0.0 copy-start.3
  209.0 3.5 %exponential_convert_fusion.1 = (bf16[128,8192]{1,0:T(8,128)(2,1)S(1)}, bf16[128,8192]{1,0:T(8,128)(2,1)S(1)}) fusion(f32[128,8192]{1,0:T(8,128)} %copy-done, f32[128]{0:T(128)S(1)} %log_add_fusion, f32[8192]{0:T(1024)S(1)} %bitcast.25), kind=kLoop, calls=%fused_computation.7 | loop fusion | flops 4194304 | bytes 8421888 | tf_op jit(solution)/shard_map/convert_element_type | solution.py:43
  212.5 0.0 copy-done.5
  212.5 0.0 copy-done.3
  212.5 0.0 copy-start.2
  212.5 1.2 fusion
  213.8 0.0 copy-done.2
  213.8 0.8 fusion.6
  (3 shorter events, 0.0 us)
Async XLA Ops:
  7.2 165.3 %all-gather.2.cloned.1.call-start = ((), (), s32[]{:S(2)}) async-start(), calls=%async_computation.1 | async-start | bytes 4259840 | tf_op jit(solution)/shard_map/all_gather | solution.py:41
  7.2 7.5 %collective-permute-start = (bf16[128,256]{1,0:T(8,128)(2,1)}, bf16[128,256]{1,0:T(8,128)(2,1)S(1)}, u32[]{:S(2)}, u32[]{:S(2)}) collective-permute-start(bf16[128,256]{1,0:T(8,128)(2,1)} %bitcast.24), channel_id=1, source_target_pairs={{0,256},{64,320},{128,384},{192,448},{256,0},{320,64},{384,128},{4... | collective-permute-start | bytes 196616 | tf_op jit(solution)/shard_map/ppermute | solution.py:10
  14.7 0.6 copy-start.1
  176.3 2.0 copy-start
  176.3 7.4 %copy-start.4 = (bf16[1,128,256]{2,1,0:T(8,128)(2,1)S(1)}, bf16[1,128,256]{2,1,0:T(8,128)(2,1)}, u32[]{:S(2)}) copy-start(bf16[1,128,256]{2,1,0:T(8,128)(2,1)} %param.2) | copy-start | bytes 196612
  179.0 33.5 %copy-start.5 = (f32[128]{0:T(128)}, f32[128]{0:T(128)S(1)}, u32[]{:S(2)}) copy-start(f32[128]{0:T(128)S(1)} %log_add_fusion) | copy-start | bytes 1540
  179.0 5.8 %collective-permute-start.1 = (f32[128]{0:T(128)S(1)}, f32[128]{0:T(128)S(1)}, u32[]{:S(2)}, u32[]{:S(2)}) collective-permute-start(f32[128]{0:T(128)S(1)} %log_add_fusion), channel_id=1, source_target_pairs={{0,256},{64,320},{128,384},{192,448},{256,0},{320,64},{384,128},{4... | collective-permute-start | bytes 1544 | tf_op jit(solution)/shard_map/ppermute | solution.py:10
  185.5 23.6 %all-to-all-start = ((f32[64,1,128]{2,1,0:T(1,128)}), f32[64,1,128]{2,1,0:T(1,128)S(1)}, u32[]{:S(2)}, u32[]{:S(2)}) async-start(f32[64,1,128]{2,1,0:T(1,128)} %stack.2), calls=%async_computation | async-start | bytes 65536 | tf_op jit(solution)/shard_map/all_to_all | solution.py:39
  209.0 3.5 %copy-start.3 = (bf16[8192,256]{1,0:T(8,128)(2,1)S(1)}, bf16[8192,256]{1,0:T(8,128)(2,1)}, u32[]{:S(2)}) copy-start(bf16[8192,256]{1,0:T(8,128)(2,1)} %all-gather.2.cloned.1.call-done) | copy-start | bytes 12582916
  212.5 1.3 copy-start.2
Sparse Core Ops, SparseCore 0:
  15.5 156.9 all-gather.1
